TPU v7x, 32 devices: a whole 2x2x4 slice. The times are simulated.
32 devices in a mesh: grp: 4 (over x, core), ctx: 4 (over z), wt: 2 (over y).
Axes of the slice: x: 2, y: 2, z: 4, core: 2. Of those that a mesh axis runs over, the one named last changes fastest.
Arguments:
- tokens: bfloat16 [8, 2048, 1280], P(('grp', 'wt'), 'ctx'), may hold values from -6 to 6
- segments: int32 [8, 2048], P(('grp', 'wt')), may hold values from 0 to 2, as said below
- w_qkv: bfloat16 [1280, 3840], P('wt'), may hold values from -0.15625 to 0.15625
- w_proj: bfloat16 [1280, 1280], P('wt'), may hold values from -1.25 to 1.25
- w_in: bfloat16 [1280, 1280], P('wt'), may hold values from -0.15625 to 0.15625
- w_out: bfloat16 [1280, 1280], P('wt'), may hold values from -0.15625 to 0.15625
- gain_attn: float32 [1280], replicated, may hold values from 0.5 to 1.5
- gain_mlp: float32 [1280], replicated, may hold values from 0.5 to 1.5
- query_scale: float32 [80], replicated, may hold values from -0.5 to 1.5
- cotangent: bfloat16 [8, 2048, 1280], P(('grp', 'wt'), 'ctx'), may hold values from -6 to 6
Outputs:
- layer_out: bfloat16 [8, 2048, 1280], P(('grp', 'wt'), 'ctx')
- grad_tokens: bfloat16 [8, 2048, 1280], P(('grp', 'wt'), 'ctx')
- grad_w_qkv: float32 [1280, 3840], P('wt')
- grad_w_proj: float32 [1280, 1280], P('wt')
- grad_w_in: float32 [1280, 1280], P('wt')
- grad_w_out: float32 [1280, 1280], P('wt')
- grad_gain_attn: float32 [1280], replicated
- grad_gain_mlp: float32 [1280], replicated
- grad_query_scale: float32 [80], replicated
Inputs may be any that keep to these rules, and one draw needn't show every extreme that they name: `segments`: in each group the id starts at 0, never falls, and every id of 0 to 2 is used. Segment 0 ends 1024 - r tokens into the group, r below 256; each later continuation starts 512 + j tokens after the one before, j within 128 either way; the last runs to the group's end.
All inputs are finite; a program needn't handle non-finite values.
Results may differ from a plain program's by a relative error of at most 0.02.
Values may be sent and summed in bfloat16 or wider, within the bound.
No kernel may reach another device: no remote copies, remote signals or barrier semaphores. Data moves between devices by JAX's collectives and lax.ppermute only.
A program may use at most 256 MiB of HBM per device.

v0:
```python
import math
import jax
import jax.numpy as jnp
from jax import lax
from jax.sharding import PartitionSpec as P

D = 1280
H = 16
HD = 80
epsilon = 1e-06
scale_base = 1.442695041
masked_fill = -1e30


def rms_inverse(values):
    return lax.rsqrt(jnp.mean(values * values, axis=-1, keepdims=True) + epsilon)


def norm_back(values, inverse, grad_scaled):
    return inverse * grad_scaled - values * (inverse * inverse * inverse) * jnp.mean(
        grad_scaled * values, axis=-1, keepdims=True
    )


def times_trans(left, right):
    return lax.dot_general(
        left, right, (((1,), (1,)), ((), ())), preferred_element_type=jnp.float32
    )


def trans_times(left, right):
    return lax.dot_general(
        left, right, (((0,), (0,)), ((), ())), preferred_element_type=jnp.float32
    )


def visible(query_pos, query_seg, seg_row, offset, key_count):
    key_pos = offset + jnp.arange(key_count, dtype=jnp.int32)
    key_seg = lax.dynamic_slice_in_dim(seg_row, offset, key_count)
    return (key_pos[None, :] <= query_pos[:, None]) & (
        (key_seg[None, :] == 0) | (key_seg[None, :] == query_seg[:, None])
    )


def blocked(step_fn, carried, shard_rows):
    length = shard_rows.shape[0]
    width = math.gcd(length, 512)

    def advance(counter, carried_in):
        beginning = counter * width
        subrows = lax.dynamic_slice_in_dim(shard_rows, beginning, width, 0)
        return step_fn(carried_in, subrows, beginning)

    return lax.fori_loop(0, length // width, advance, carried)


def local(
    tokens, segments, w_qkv, w_proj, w_in, w_out, gain_attn, gain_mlp, query_scale, cotangent
):
    inputs = tokens[0].astype(jnp.float32)
    rows = inputs.shape[0]
    seg_row = segments[0]
    group_len = seg_row.shape[0]
    own_index = lax.axis_index("ctx")
    own_offset = own_index * rows
    query_pos = own_offset + jnp.arange(rows, dtype=jnp.int32)
    query_seg = lax.dynamic_slice_in_dim(seg_row, own_offset, rows)
    full_qkv, full_proj, full_in, full_out = (
        lax.all_gather(w_qkv, "wt", axis=0, tiled=True),
        lax.all_gather(w_proj, "wt", axis=0, tiled=True),
        lax.all_gather(w_in, "wt", axis=0, tiled=True),
        lax.all_gather(w_out, "wt", axis=0, tiled=True),
    )
    inverse_attn = rms_inverse(inputs)
    normed = (inputs * inverse_attn * gain_attn).astype(jnp.bfloat16)
    project = jnp.dot(normed, full_qkv, preferred_element_type=jnp.float32)
    dim_scale = scale_base / math.sqrt(HD) * jax.nn.softplus(query_scale)
    raw_queries = project[:, :D].reshape(rows, H, HD)
    queries = (raw_queries * dim_scale).astype(jnp.bfloat16)
    keyval = project[:, D:].astype(jnp.bfloat16)

    def forward_step(carried, subrows, offset):
        running_max, running_sum, accum = carried
        key_count = subrows.shape[0]
        keys_part = subrows[:, :D].reshape(key_count, H, HD)
        values_part = subrows[:, D:].reshape(key_count, H, HD)
        scores = jnp.einsum("qhd,khd->hqk", queries, keys_part, preferred_element_type=jnp.float32)
        allowed = visible(query_pos, query_seg, seg_row, offset, key_count)[None]
        masked = jnp.where(allowed, scores, masked_fill)
        new_max = jnp.maximum(running_max, jnp.max(masked, axis=-1))
        factor = jnp.exp(running_max - new_max)
        exponent = jnp.where(allowed, jnp.exp(masked - new_max[:, :, None]), 0.0)
        running_sum = running_sum * factor + jnp.sum(exponent, axis=-1)
        accum = accum * jnp.transpose(factor)[:, :, None] + jnp.einsum(
            "hqk,khd->qhd",
            exponent.astype(jnp.bfloat16),
            values_part,
            preferred_element_type=jnp.float32,
        )
        return (new_max, running_sum, accum)

    start_state = (
        jnp.full((H, rows), masked_fill, jnp.float32),
        jnp.zeros((H, rows), jnp.float32),
        jnp.zeros((rows, H, HD), jnp.float32),
    )
    running_max, running_sum, accum = blocked(
        forward_step, start_state, lax.all_gather(keyval, "ctx", axis=0, tiled=True)
    )
    logsum = running_max + jnp.log(running_sum)
    attn_float = accum / jnp.transpose(running_sum)[:, :, None]
    attended = attn_float.reshape(rows, D).astype(jnp.bfloat16)
    resid = inputs + jnp.dot(attended, full_proj, preferred_element_type=jnp.float32)
    inverse_mlp = rms_inverse(resid)
    normed_mlp = (resid * inverse_mlp * gain_mlp).astype(jnp.bfloat16)
    hidden = jnp.dot(normed_mlp, full_in, preferred_element_type=jnp.float32)
    active = jax.nn.silu(hidden).astype(jnp.bfloat16)
    layer_out = (resid + jnp.dot(active, full_out, preferred_element_type=jnp.float32)).astype(
        jnp.bfloat16
    )
    back_qkv, back_proj, back_in, back_out = (
        lax.all_gather(w_qkv, "wt", axis=0, tiled=True),
        lax.all_gather(w_proj, "wt", axis=0, tiled=True),
        lax.all_gather(w_in, "wt", axis=0, tiled=True),
        lax.all_gather(w_out, "wt", axis=0, tiled=True),
    )
    grad_out = cotangent[0].astype(jnp.float32)
    grad_mlp = cotangent[0]
    grad_active = times_trans(grad_mlp, back_out)
    grad_w_out = trans_times(active, grad_mlp)
    sigmoid_h = jax.nn.sigmoid(hidden)
    grad_hidden = (grad_active * sigmoid_h * (1.0 + hidden * (1.0 - sigmoid_h))).astype(
        jnp.bfloat16
    )
    grad_w_in = trans_times(normed_mlp, grad_hidden)
    grad_normed_mlp = times_trans(grad_hidden, back_in)
    grad_gain_mlp = jnp.sum(grad_normed_mlp * resid * inverse_mlp, axis=0)
    grad_resid = grad_out + norm_back(resid, inverse_mlp, grad_normed_mlp * gain_mlp)
    grad_proj = grad_resid.astype(jnp.bfloat16)
    grad_w_proj = trans_times(attended, grad_proj)
    grad_attended = times_trans(grad_proj, back_proj).astype(jnp.bfloat16).reshape(rows, H, HD)
    delta = jnp.transpose(jnp.sum(grad_attended.astype(jnp.float32) * attn_float, axis=-1))

    def backward_step(carried, subrows, offset):
        grad_queries, grad_keyval = carried
        key_count = subrows.shape[0]
        keys_part = subrows[:, :D].reshape(key_count, H, HD)
        values_part = subrows[:, D:].reshape(key_count, H, HD)
        scores = jnp.einsum("qhd,khd->hqk", queries, keys_part, preferred_element_type=jnp.float32)
        allowed = visible(query_pos, query_seg, seg_row, offset, key_count)[None]
        probs = jnp.where(
            allowed, jnp.exp(jnp.where(allowed, scores, masked_fill) - logsum[:, :, None]), 0.0
        )
        grad_probs = jnp.einsum(
            "qhd,khd->hqk", grad_attended, values_part, preferred_element_type=jnp.float32
        )
        grad_scores = (probs * (grad_probs - delta[:, :, None])).astype(jnp.bfloat16)
        grad_queries = grad_queries + jnp.einsum(
            "hqk,khd->qhd", grad_scores, keys_part, preferred_element_type=jnp.float32
        )
        grad_keys = jnp.einsum(
            "hqk,qhd->khd", grad_scores, queries, preferred_element_type=jnp.float32
        )
        grad_values = jnp.einsum(
            "hqk,qhd->khd",
            probs.astype(jnp.bfloat16),
            grad_attended,
            preferred_element_type=jnp.float32,
        )
        combined = jnp.concatenate(
            [grad_keys.reshape(key_count, D), grad_values.reshape(key_count, D)], axis=1
        )
        current = lax.dynamic_slice_in_dim(grad_keyval, offset, key_count, 0)
        grad_keyval = lax.dynamic_update_slice_in_dim(grad_keyval, current + combined, offset, 0)
        return (grad_queries, grad_keyval)

    back_state = (jnp.zeros((rows, H, HD), jnp.float32), jnp.zeros((group_len, 2 * D), jnp.float32))
    grad_queries, grad_keyval = blocked(
        backward_step, back_state, lax.all_gather(keyval, "ctx", axis=0, tiled=True)
    )
    grad_keyval_own = lax.psum_scatter(
        grad_keyval.astype(jnp.bfloat16), "ctx", scatter_dimension=0, tiled=True
    ).astype(jnp.float32)
    grad_dims = jnp.sum(grad_queries * raw_queries, axis=(0, 1))
    grad_query_scale = grad_dims * (scale_base / math.sqrt(HD)) * jax.nn.sigmoid(query_scale)
    grad_project = jnp.concatenate(
        [(grad_queries * dim_scale).reshape(rows, D), grad_keyval_own], axis=1
    ).astype(jnp.bfloat16)
    grad_w_qkv = trans_times(normed, grad_project)
    grad_normed = times_trans(grad_project, back_qkv)
    grad_gain_attn = jnp.sum(grad_normed * inputs * inverse_attn, axis=0)
    grad_tokens = (grad_resid + norm_back(inputs, inverse_attn, grad_normed * gain_attn)).astype(
        jnp.bfloat16
    )
    shard_qkv, shard_proj, shard_in, shard_out = (
        lax.psum_scatter(
            grad_w_qkv.astype(jnp.bfloat16), "wt", scatter_dimension=0, tiled=True
        ).astype(jnp.float32),
        lax.psum_scatter(
            grad_w_proj.astype(jnp.bfloat16), "wt", scatter_dimension=0, tiled=True
        ).astype(jnp.float32),
        lax.psum_scatter(
            grad_w_in.astype(jnp.bfloat16), "wt", scatter_dimension=0, tiled=True
        ).astype(jnp.float32),
        lax.psum_scatter(
            grad_w_out.astype(jnp.bfloat16), "wt", scatter_dimension=0, tiled=True
        ).astype(jnp.float32),
    )
    total_qkv, total_proj, total_in, total_out = (
        lax.psum(shard_qkv.astype(jnp.bfloat16), ("grp", "ctx")).astype(jnp.float32),
        lax.psum(shard_proj.astype(jnp.bfloat16), ("grp", "ctx")).astype(jnp.float32),
        lax.psum(shard_in.astype(jnp.bfloat16), ("grp", "ctx")).astype(jnp.float32),
        lax.psum(shard_out.astype(jnp.bfloat16), ("grp", "ctx")).astype(jnp.float32),
    )
    total_gain_attn, total_gain_mlp, total_scale = lax.psum(
        (grad_gain_attn, grad_gain_mlp, grad_query_scale), ("grp", "ctx", "wt")
    )
    return (
        layer_out[None],
        grad_tokens[None],
        total_qkv,
        total_proj,
        total_in,
        total_out,
        total_gain_attn,
        total_gain_mlp,
        total_scale,
    )


def solution(mesh):
    placed = (
        P(("grp", "wt"), "ctx", None),
        P(("grp", "wt"), None),
        P("wt", None),
        P("wt", None),
        P("wt", None),
        P("wt", None),
        P(),
        P(),
        P(),
        P(("grp", "wt"), "ctx", None),
    )
    return jax.shard_map(
        local,
        mesh=mesh,
        in_specs=placed,
        out_specs=(
            P(("grp", "wt"), "ctx", None),
            P(("grp", "wt"), "ctx", None),
            P("wt", None),
            P("wt", None),
            P("wt", None),
            P("wt", None),
            P(),
            P(),
            P(),
        ),
        check_vma=False,
    )
```

profile of v0, /device:TPU:0, one launch (start us, length us, event | category | flops | bytes accessed | tf_op | source)
XLA Modules:
  0.0 1364.7 jit_solution(8203904737533730321)
XLA Ops:
  9.4 125.2 %all-gather.6.cloned.1.call-done = bf16[1280,3840]{1,0:T(8,128)(2,1)} async-done(((bf16[640,3840]{1,0:T(8,128)(2,1)}), bf16[1280,3840]{1,0:T(8,128)(2,1)}) %all-gather.6.cloned.1.call-update) | async-done | bytes 9830416 | tf_op jit(solution)/shard_map/all_gather | solution.py:69
  156.0 175.5 %all-gather.8.cloned.1.call-done = bf16[2048,2560]{1,0:T(8,128)(2,1)} async-done(((bf16[512,2560]{1,0:T(8,128)(2,1)}), bf16[2048,2560]{1,0:T(8,128)(2,1)}) %all-gather.8.cloned.1.call-update) | async-done | bytes 10485776 | tf_op jit(solution)/shard_map/all_gather | solution.py:108
  331.5 14.6 %copy.34 = bf16[2048,2560]{0,1:T(8,128)(2,1)} copy(bf16[2048,2560]{1,0:T(8,128)(2,1)} %all-gather.8.cloned.1.call-done) | data formatting | bytes 20971520
  346.1 122.1 %while.34 = (s32[]{:T(128)}, f32[16,512]{1,0:T(8,128)S(1)}, f32[16,512]{1,0:T(8,128)S(1)}, f32[512,16,80]{0,2,1:T(8,128)}, s32[2048]{0:T(1024)S(1)}, /*index=5*/...) while((s32[]{:T(128)}, f32[16,512]{1,0:T(8,128)S(1)}, ...), condition=%wide.region_4.5_spmd.clone, body=%wide.region_1.4_spmd.clone.sunk | while | flops 1387185664 | bytes 66340068 | solution.py:54
  356.6 9.2 fusion.115
  365.8 9.7 bitcast_add_fusion.4
  386.8 10.0 fusion.115
  396.7 10.4 bitcast_add_fusion.4
  417.8 9.2 fusion.115
  427.0 10.7 bitcast_add_fusion.4
  448.4 9.2 fusion.115
  457.5 10.4 bitcast_add_fusion.4
  500.7 9.7 broadcast_in_dim.141
  510.4 188.2 %while.35 = (s32[]{:T(128)}, f32[512,16,80]{0,2,1:T(8,128)}, f32[2048,2560]{0,1:T(8,128)}, bf16[2048,2560]{0,1:T(8,128)(2,1)}, s32[2048]{0:T(1024)S(1)}, /*index...) while((s32[]{:T(128)}, f32[512,16,80]{0,2,1:T(8,128)}, ...), condition=%wide.region_9.10_spmd.clone, body=%wide.region_8.9_spmd.clone.sunk | while | flops 3402368512 | bytes 138003792 | solution.py:54
  523.4 11.4 fusion.130
  534.8 9.7 fusion.129
  569.0 11.4 fusion.130
  580.4 9.7 fusion.129
  616.4 11.4 fusion.130
  627.8 9.7 fusion.129
  663.7 11.4 fusion.130
  675.1 9.7 fusion.129
  698.6 12.3 convert_element_type.118
  736.2 151.1 %reduce-scatter.6.cloned.1.call-done = bf16[512,2560]{0,1:T(8,128)(2,1)} async-done(((bf16[2048,2560]{0,1:T(8,128)(2,1)}), bf16[512,2560]{0,1:T(8,128)(2,1)}) %reduce-scatter.6.cloned.1.call-update) | async-done | bytes 2621456 | tf_op jit(solution)/shard_map/reduce_scatter | solution.py:181
  887.3 10.9 convolution_convert_fusion
  898.4 37.5 %reduce-scatter.12.cloned.1.call-done = bf16[640,1280]{1,0:T(8,128)(2,1)} async-done(((bf16[1280,1280]{1,0:T(8,128)(2,1)}), bf16[640,1280]{1,0:T(8,128)(2,1)}) %reduce-scatter.12.cloned.1.call-update) | async-done | bytes 1638416 | tf_op jit(solution)/shard_map/reduce_scatter | solution.py:202
  936.0 47.7 %reduce-scatter.14.cloned.1.call-done = bf16[640,1280]{1,0:T(8,128)(2,1)} async-done(((bf16[1280,1280]{1,0:T(8,128)(2,1)}), bf16[640,1280]{1,0:T(8,128)(2,1)}) %reduce-scatter.14.cloned.1.call-update) | async-done | bytes 1638416 | tf_op jit(solution)/shard_map/reduce_scatter | solution.py:205
  983.7 47.6 %reduce-scatter.10.cloned.1.call-done = bf16[640,1280]{1,0:T(8,128)(2,1)} async-done(((bf16[1280,1280]{1,0:T(8,128)(2,1)}), bf16[640,1280]{1,0:T(8,128)(2,1)}) %reduce-scatter.10.cloned.1.call-update) | async-done | bytes 1638416 | tf_op jit(solution)/shard_map/reduce_scatter | solution.py:199
  1031.3 117.7 %reduce-scatter.8.cloned.1.call-done = bf16[640,3840]{1,0:T(8,128)(2,1)} async-done(((bf16[1280,3840]{1,0:T(8,128)(2,1)}), bf16[640,3840]{1,0:T(8,128)(2,1)}) %reduce-scatter.8.cloned.1.call-update) | async-done | bytes 4915216 | tf_op jit(solution)/shard_map/reduce_scatter | solution.py:196
  1156.6 12.2 fusion.40
  1168.8 41.6 %all-reduce = (f32[1280]{0:T(1024)}, f32[1280]{0:T(1024)}, f32[80]{0:T(128)}) all-reduce(f32[1280]{0:T(1024)S(1)} %get-tuple-element.469, f32[1280]{0:T(1024)S(1)} %copy-done.24, f32[80]{0:T(128)S(1)} %divide_multiply_fusion), channel_id=1, replica_groups=mesh['grp'=4,'ctx'=4,'wt'=2] {'grp','ctx','wt'}, use_global_device_ids=true, to_apply=%region_21.22 | all-reduce | flops 2640 | bytes 21120 | tf_op jit(solution)/shard_map/psum | solution.py:215
  1214.8 131.1 %all-reduce.4.cloned.1.call-done = (bf16[640,3840]{1,0:T(8,128)(2,1)}, bf16[640,1280]{1,0:T(8,128)(2,1)}, bf16[640,1280]{1,0:T(8,128)(2,1)}, bf16[640,1280]{1,0:T(8,128)(2,1)}) async-done(((bf16[640,3840]{1,0:T(8,128)(2,1)}, bf16[640,1280]{1,0:T(8,128)(2,1)}, bf16[640,1280]{1,0:T(8,128)(2,1)}, bf16[640,1280]{1,0:T(8,128)(2,1)}), (bf16[640,3840]{1,0:T(8,128)(2,1)}, bf16[640,1280]{1,0:T(8,128)(2,1)}, ...) | async-done | bytes 9830416 | tf_op jit(solution)/shard_map/psum | solution.py:210
  (222 shorter events, 251.4 us)
Async XLA Ops:
  7.2 127.5 %copy-start.19 = (f32[1280]{0:T(1024)S(1)}, f32[1280]{0:T(1024)}, u32[]{:S(2)}) copy-start(f32[1280]{0:T(1024)} %param.20) | copy-start | bytes 15364
  7.2 127.4 %all-gather.6.cloned.1.call-start = ((), (), s32[]{:S(2)}) async-start(), calls=%async_computation.5 | async-start | bytes 14745600 | tf_op jit(solution)/shard_map/all_gather | solution.py:69
  7.9 323.5 %all-gather.8.cloned.1.call-start = ((), (), s32[]{:S(2)}) async-start(), calls=%async_computation.6 | async-start | bytes 13107200 | tf_op jit(solution)/shard_map/all_gather | solution.py:108
  9.4 132.9 %copy-start.22 = (f32[512]{0:T(512)}, f32[512]{0:T(512)S(1)}, u32[]{:S(2)}) copy-start(f32[512]{0:T(512)S(1)} %get-tuple-element.537) | copy-start | bytes 6148
  147.4 324.1 %all-gather.10.cloned.1.call-start = ((), (), s32[]{:S(2)}) async-start(), calls=%async_computation.7 | async-start | bytes 4915200 | tf_op jit(solution)/shard_map/all_gather | solution.py:70
  148.1 329.2 %all-gather.12.cloned.1.call-start = ((), (), s32[]{:S(2)}) async-start(), calls=%async_computation.8 | async-start | bytes 4915200 | tf_op jit(solution)/shard_map/all_gather | solution.py:71
  148.7 334.9 %all-gather.14.cloned.1.call-start = ((), (), s32[]{:S(2)}) async-start(), calls=%async_computation.9 | async-start | bytes 4915200 | tf_op jit(solution)/shard_map/all_gather | solution.py:72
  149.3 738.0 %reduce-scatter.6.cloned.1.call-start = ((), (), s32[]{:S(2)}) async-start(), calls=%async_computation.10 | async-start | bytes 13107200 | tf_op jit(solution)/shard_map/reduce_scatter | solution.py:181
  149.6 3.9 copy-start.29
  471.5 5.9 copy-start.25
  477.3 14.2 %copy-start.27 = (f32[512]{0:T(512)}, f32[512]{0:T(512)S(1)}, u32[]{:S(2)}) copy-start(f32[512]{0:T(512)S(1)} %get-tuple-element.539) | copy-start | bytes 6148
  477.3 6.3 copy-start.16
  483.6 5.1 copy-start.6
  483.6 5.1 copy-start.31
  550.2 6.2 copy-start.12
  597.5 6.3 copy-start.12
  644.9 6.2 copy-start.12
  692.2 6.2 copy-start.12
  710.9 225.1 %reduce-scatter.12.cloned.1.call-start = ((), (), s32[]{:S(2)}) async-start(), calls=%async_computation.13 | async-start | bytes 4915200 | tf_op jit(solution)/shard_map/reduce_scatter | solution.py:202
  717.6 266.1 %reduce-scatter.14.cloned.1.call-start = ((), (), s32[]{:S(2)}) async-start(), calls=%async_computation.14 | async-start | bytes 4915200 | tf_op jit(solution)/shard_map/reduce_scatter | solution.py:205
  724.4 307.0 %reduce-scatter.10.cloned.1.call-start = ((), (), s32[]{:S(2)}) async-start(), calls=%async_computation.12 | async-start | bytes 4915200 | tf_op jit(solution)/shard_map/reduce_scatter | solution.py:199
  731.0 418.0 %reduce-scatter.8.cloned.1.call-start = ((), (), s32[]{:S(2)}) async-start(), calls=%async_computation.11 | async-start | bytes 14745600 | tf_op jit(solution)/shard_map/reduce_scatter | solution.py:196
  732.7 154.6 %copy-start.20 = (f32[1280]{0:T(1024)S(1)}, f32[1280]{0:T(1024)}, u32[]{:S(2)}) copy-start(f32[1280]{0:T(1024)} %param.20) | copy-start | bytes 15364
  732.7 154.6 %copy-start.23 = (f32[512]{0:T(512)S(1)}, f32[512]{0:T(512)}, u32[]{:S(2)}) copy-start(f32[512]{0:T(512)} %copy-done.22) | copy-start | bytes 6148
  898.2 447.7 %all-reduce.4.cloned.1.call-start = ((), (), s32[]{:S(2)}) async-start(), calls=%async_computation.15 | async-start | bytes 19660800 | tf_op jit(solution)/shard_map/psum | solution.py:210
  1149.7 6.9 copy-start.4
  1149.7 6.9 copy-start.15
  1149.7 6.9 copy-start.32
  1156.6 12.2 copy-start.24
  1156.6 53.8 %copy-start.21 = (f32[512]{0:T(512)S(1)}, f32[512]{0:T(512)}, u32[]{:S(2)}) copy-start(f32[512]{0:T(512)} %get-tuple-element.536) | copy-start | bytes 6148
  1345.9 7.5 slice-start.1
  1349.4 3.9 slice-start.2
  (27 other events, 53.3 us)
Sparse Core Ops, SparseCore 0:
  9.6 125.0 all-gather.5
  147.5 183.9 all-gather.7
  333.0 44.5 all-gather.9
  379.0 46.4 all-gather.11
  426.9 46.3 all-gather.13
  711.0 176.2 reduce-scatter.5
  890.1 45.8 reduce-scatter.11
  938.9 44.7 reduce-scatter.13
  986.5 44.7 reduce-scatter.9
  1034.2 114.7 reduce-scatter.7
  1153.0 192.8 all-reduce.3
where the time goes:
time: 1370 us; the launch traced here: 1360 us
  waiting for transfers between devices  836 us (61%)
  matrix products  296 us (22%)
  other arithmetic  108 us (8%)
  local copies, waits for them, and re-layouts  67.2 us (5%)
  blocking collectives  41.6 us (3%)
  between operations  14.5 us (1%)
    all_gather x1, waiting for transfers between devices, local(): lax.all_gather(keyval, 'ctx', axis=0, tiled=True)  175 us
    reduce_scatter x1, waiting for transfers between devices, local(): lax.psum_scatter(grad_keyval.astype(jnp.bfloat16), 'ctx', scatter_dimensi...  151 us
    psum x1, waiting for transfers between devices, local(): lax.psum(shard_qkv.astype(jnp.bfloat16), ('grp', 'ctx')).astype(jnp.float32)  131 us
    all_gather x1, waiting for transfers between devices, local(): lax.all_gather(w_qkv, 'wt', axis=0, tiled=True)  125 us
    reduce_scatter x1, waiting for transfers between devices, local(): lax.psum_scatter(grad_w_qkv.astype(jnp.bfloat16), 'wt', scatter_dimension...  118 us
    reduce_scatter x1, waiting for transfers between devices, local(): lax.psum_scatter(grad_w_out.astype(jnp.bfloat16), 'wt', scatter_dimension...  47.7 us
    reduce_scatter x1, waiting for transfers between devices, local(): lax.psum_scatter(grad_w_proj.astype(jnp.bfloat16), 'wt', scatter_dimensio...  47.6 us
    dot_general x4, matrix products, backward_step(): jnp.einsum('hqk,qhd->khd', probs.astype(jnp.bfloat16), grad_attended, pre...  45.8 us
  transfers between devices with their start and end apart: 11, of which 8 were waited for; matrix products, arithmetic and copies ran while one was open for 15% of the time, Pallas kernels for 0%

commit v1 on v0

--- a/solution.py
+++ b/solution.py
@@ -213,7 +213,7 @@
         lax.psum(shard_out.astype(jnp.bfloat16), ("grp", "ctx")).astype(jnp.float32),
     )
     total_gain_attn, total_gain_mlp, total_scale = lax.psum(
-        (grad_gain_attn, grad_gain_mlp, grad_query_scale), ("grp", "ctx", "wt")
+        lax.psum((grad_gain_attn, grad_gain_mlp, grad_query_scale), "grp"), ("ctx", "wt")
     )
     return (
         layer_out[None],

time: 1370 us -> 1370 us (level)
    psum x1 -> x2, blocking collectives: 41.6 us -> 50.6 us  [the longest x1 38.2 us: local(): lax.psum(lax.psum((grad_gain_attn, grad_gain_mlp, grad_query_scale), 'grp...]
where the time goes in v1:
time: 1370 us; the launch traced here: 1360 us
  waiting for transfers between devices  827 us (60%)
  matrix products  296 us (22%)
  other arithmetic  108 us (8%)
  local copies, waits for them, and re-layouts  67.2 us (5%)
  blocking collectives  50.6 us (4%)
  between operations  14.5 us (1%)
    all_gather x1, waiting for transfers between devices, local(): lax.all_gather(keyval, 'ctx', axis=0, tiled=True)  175 us
    reduce_scatter x1, waiting for transfers between devices, local(): lax.psum_scatter(grad_keyval.astype(jnp.bfloat16), 'ctx', scatter_dimensi...  151 us
    all_gather x1, waiting for transfers between devices, local(): lax.all_gather(w_qkv, 'wt', axis=0, tiled=True)  125 us
    psum x1, waiting for transfers between devices, local(): lax.psum(shard_qkv.astype(jnp.bfloat16), ('grp', 'ctx')).astype(jnp.float32)  122 us
    reduce_scatter x1, waiting for transfers between devices, local(): lax.psum_scatter(grad_w_qkv.astype(jnp.bfloat16), 'wt', scatter_dimension...  118 us
    reduce_scatter x1, waiting for transfers between devices, local(): lax.psum_scatter(grad_w_out.astype(jnp.bfloat16), 'wt', scatter_dimension...  47.7 us
    reduce_scatter x1, waiting for transfers between devices, local(): lax.psum_scatter(grad_w_proj.astype(jnp.bfloat16), 'wt', scatter_dimensio...  47.6 us
    dot_general x4, matrix products, backward_step(): jnp.einsum('hqk,qhd->khd', probs.astype(jnp.bfloat16), grad_attended, pre...  45.8 us
  transfers between devices with their start and end apart: 11, of which 8 were waited for; matrix products, arithmetic and copies ran while one was open for 15% of the time, Pallas kernels for 0%

profile of v1, /device:TPU:0, one launch (start us, length us, event | category | flops | bytes accessed | tf_op | source)
XLA Modules:
  0.0 1364.5 jit_solution(1910236720841409726)
XLA Ops:
  9.4 125.2 %all-gather.6.cloned.1.call-done = bf16[1280,3840]{1,0:T(8,128)(2,1)} async-done(((bf16[640,3840]{1,0:T(8,128)(2,1)}), bf16[1280,3840]{1,0:T(8,128)(2,1)}) %all-gather.6.cloned.1.call-update) | async-done | bytes 9830416 | tf_op jit(solution)/shard_map/all_gather | solution.py:69
  156.0 175.5 %all-gather.8.cloned.1.call-done = bf16[2048,2560]{1,0:T(8,128)(2,1)} async-done(((bf16[512,2560]{1,0:T(8,128)(2,1)}), bf16[2048,2560]{1,0:T(8,128)(2,1)}) %all-gather.8.cloned.1.call-update) | async-done | bytes 10485776 | tf_op jit(solution)/shard_map/all_gather | solution.py:108
  331.5 14.7 %copy.34 = bf16[2048,2560]{0,1:T(8,128)(2,1)} copy(bf16[2048,2560]{1,0:T(8,128)(2,1)} %all-gather.8.cloned.1.call-done) | data formatting | bytes 20971520
  346.1 122.2 %while.34 = (s32[]{:T(128)}, f32[16,512]{1,0:T(8,128)S(1)}, f32[16,512]{1,0:T(8,128)S(1)}, f32[512,16,80]{0,2,1:T(8,128)}, s32[2048]{0:T(1024)S(1)}, /*index=5*/...) while((s32[]{:T(128)}, f32[16,512]{1,0:T(8,128)S(1)}, ...), condition=%wide.region_4.5_spmd.clone, body=%wide.region_1.4_spmd.clone.sunk | while | flops 1387185664 | bytes 66340068 | solution.py:54
  356.7 9.2 fusion.115
  365.9 9.7 bitcast_add_fusion.4
  386.9 9.9 fusion.115
  396.8 10.4 bitcast_add_fusion.4
  417.9 9.2 fusion.115
  427.1 10.8 bitcast_add_fusion.4
  457.6 10.4 bitcast_add_fusion.4
  500.8 9.7 broadcast_in_dim.141
  510.5 188.1 %while.35 = (s32[]{:T(128)}, f32[512,16,80]{0,2,1:T(8,128)}, f32[2048,2560]{0,1:T(8,128)}, bf16[2048,2560]{0,1:T(8,128)(2,1)}, s32[2048]{0:T(1024)S(1)}, /*index...) while((s32[]{:T(128)}, f32[512,16,80]{0,2,1:T(8,128)}, ...), condition=%wide.region_9.10_spmd.clone, body=%wide.region_8.9_spmd.clone.sunk | while | flops 3402368512 | bytes 138003792 | solution.py:54
  523.5 11.4 fusion.130
  534.9 9.7 fusion.129
  569.1 11.4 fusion.130
  580.5 9.7 fusion.129
  616.4 11.4 fusion.130
  627.8 9.7 fusion.129
  663.7 11.4 fusion.130
  675.2 9.7 fusion.129
  698.6 12.3 convert_element_type.118
  736.3 151.1 %reduce-scatter.6.cloned.1.call-done = bf16[512,2560]{0,1:T(8,128)(2,1)} async-done(((bf16[2048,2560]{0,1:T(8,128)(2,1)}), bf16[512,2560]{0,1:T(8,128)(2,1)}) %reduce-scatter.6.cloned.1.call-update) | async-done | bytes 2621456 | tf_op jit(solution)/shard_map/reduce_scatter | solution.py:181
  887.4 10.9 convolution_convert_fusion
  898.5 37.5 %reduce-scatter.12.cloned.1.call-done = bf16[640,1280]{1,0:T(8,128)(2,1)} async-done(((bf16[1280,1280]{1,0:T(8,128)(2,1)}), bf16[640,1280]{1,0:T(8,128)(2,1)}) %reduce-scatter.12.cloned.1.call-update) | async-done | bytes 1638416 | tf_op jit(solution)/shard_map/reduce_scatter | solution.py:202
  936.0 47.7 %reduce-scatter.14.cloned.1.call-done = bf16[640,1280]{1,0:T(8,128)(2,1)} async-done(((bf16[1280,1280]{1,0:T(8,128)(2,1)}), bf16[640,1280]{1,0:T(8,128)(2,1)}) %reduce-scatter.14.cloned.1.call-update) | async-done | bytes 1638416 | tf_op jit(solution)/shard_map/reduce_scatter | solution.py:205
  983.8 47.6 %reduce-scatter.10.cloned.1.call-done = bf16[640,1280]{1,0:T(8,128)(2,1)} async-done(((bf16[1280,1280]{1,0:T(8,128)(2,1)}), bf16[640,1280]{1,0:T(8,128)(2,1)}) %reduce-scatter.10.cloned.1.call-update) | async-done | bytes 1638416 | tf_op jit(solution)/shard_map/reduce_scatter | solution.py:199
  1031.4 117.7 %reduce-scatter.8.cloned.1.call-done = bf16[640,3840]{1,0:T(8,128)(2,1)} async-done(((bf16[1280,3840]{1,0:T(8,128)(2,1)}), bf16[640,3840]{1,0:T(8,128)(2,1)}) %reduce-scatter.8.cloned.1.call-update) | async-done | bytes 4915216 | tf_op jit(solution)/shard_map/reduce_scatter | solution.py:196
  1156.7 12.2 fusion.40
  1168.9 12.5 all-reduce.1
  1181.3 38.2 %all-reduce = (f32[1280]{0:T(1024)}, f32[1280]{0:T(1024)}, f32[80]{0:T(128)}) all-reduce(f32[1280]{0:T(1024)S(1)} %get-tuple-element.514, f32[1280]{0:T(1024)S(1)} %get-tuple-element.515, f32[80]{0:T(128)S(1)} %get-tuple-element.516), channel_id=1, replica_groups=mesh['grp'=4,'ctx'=4,'wt'=2] {'ctx','wt'}, use_global_device_ids=true, to_apply=%region_22.23 | all-reduce | flops 2640 | bytes 21120 | tf_op jit(solution)/shard_map/psum | solution.py:215
  1223.8 121.8 %all-reduce.5.cloned.1.call-done = (bf16[640,3840]{1,0:T(8,128)(2,1)}, bf16[640,1280]{1,0:T(8,128)(2,1)}, bf16[640,1280]{1,0:T(8,128)(2,1)}, bf16[640,1280]{1,0:T(8,128)(2,1)}) async-done(((bf16[640,3840]{1,0:T(8,128)(2,1)}, bf16[640,1280]{1,0:T(8,128)(2,1)}, bf16[640,1280]{1,0:T(8,128)(2,1)}, bf16[640,1280]{1,0:T(8,128)(2,1)}), (bf16[640,3840]{1,0:T(8,128)(2,1)}, bf16[640,1280]{1,0:T(8,128)(2,1)}, ...) | async-done | bytes 9830416 | tf_op jit(solution)/shard_map/psum | solution.py:210
  (223 shorter events, 260.5 us)
Async XLA Ops:
  7.2 127.5 %copy-start.19 = (f32[1280]{0:T(1024)S(1)}, f32[1280]{0:T(1024)}, u32[]{:S(2)}) copy-start(f32[1280]{0:T(1024)} %param.20) | copy-start | bytes 15364
  7.2 127.4 %all-gather.6.cloned.1.call-start = ((), (), s32[]{:S(2)}) async-start(), calls=%async_computation.5 | async-start | bytes 14745600 | tf_op jit(solution)/shard_map/all_gather | solution.py:69
  7.9 323.5 %all-gather.8.cloned.1.call-start = ((), (), s32[]{:S(2)}) async-start(), calls=%async_computation.6 | async-start | bytes 13107200 | tf_op jit(solution)/shard_map/all_gather | solution.py:108
  9.4 132.9 %copy-start.22 = (f32[512]{0:T(512)}, f32[512]{0:T(512)S(1)}, u32[]{:S(2)}) copy-start(f32[512]{0:T(512)S(1)} %get-tuple-element.540) | copy-start | bytes 6148
  147.4 324.2 %all-gather.10.cloned.1.call-start = ((), (), s32[]{:S(2)}) async-start(), calls=%async_computation.7 | async-start | bytes 4915200 | tf_op jit(solution)/shard_map/all_gather | solution.py:70
  148.1 329.3 %all-gather.12.cloned.1.call-start = ((), (), s32[]{:S(2)}) async-start(), calls=%async_computation.8 | async-start | bytes 4915200 | tf_op jit(solution)/shard_map/all_gather | solution.py:71
  148.7 335.0 %all-gather.14.cloned.1.call-start = ((), (), s32[]{:S(2)}) async-start(), calls=%async_computation.9 | async-start | bytes 4915200 | tf_op jit(solution)/shard_map/all_gather | solution.py:72
  149.3 738.1 %reduce-scatter.6.cloned.1.call-start = ((), (), s32[]{:S(2)}) async-start(), calls=%async_computation.10 | async-start | bytes 13107200 | tf_op jit(solution)/shard_map/reduce_scatter | solution.py:181
  149.6 3.9 copy-start.29
  471.6 5.9 copy-start.25
  477.4 14.2 %copy-start.27 = (f32[512]{0:T(512)}, f32[512]{0:T(512)S(1)}, u32[]{:S(2)}) copy-start(f32[512]{0:T(512)S(1)} %get-tuple-element.542) | copy-start | bytes 6148
  477.5 6.3 copy-start.16
  483.8 5.1 copy-start.8
  483.8 5.1 copy-start.31
  550.3 6.2 copy-start.12
  597.6 6.2 copy-start.12
  644.9 6.2 copy-start.12
  692.2 6.3 copy-start.12
  710.9 225.1 %reduce-scatter.12.cloned.1.call-start = ((), (), s32[]{:S(2)}) async-start(), calls=%async_computation.13 | async-start | bytes 4915200 | tf_op jit(solution)/shard_map/reduce_scatter | solution.py:202
  717.7 266.1 %reduce-scatter.14.cloned.1.call-start = ((), (), s32[]{:S(2)}) async-start(), calls=%async_computation.14 | async-start | bytes 4915200 | tf_op jit(solution)/shard_map/reduce_scatter | solution.py:205
  724.4 307.0 %reduce-scatter.10.cloned.1.call-start = ((), (), s32[]{:S(2)}) async-start(), calls=%async_computation.12 | async-start | bytes 4915200 | tf_op jit(solution)/shard_map/reduce_scatter | solution.py:199
  731.1 418.0 %reduce-scatter.8.cloned.1.call-start = ((), (), s32[]{:S(2)}) async-start(), calls=%async_computation.11 | async-start | bytes 14745600 | tf_op jit(solution)/shard_map/reduce_scatter | solution.py:196
  732.8 154.6 %copy-start.20 = (f32[1280]{0:T(1024)S(1)}, f32[1280]{0:T(1024)}, u32[]{:S(2)}) copy-start(f32[1280]{0:T(1024)} %param.20) | copy-start | bytes 15364
  732.8 154.6 %copy-start.23 = (f32[512]{0:T(512)S(1)}, f32[512]{0:T(512)}, u32[]{:S(2)}) copy-start(f32[512]{0:T(512)} %copy-done.22) | copy-start | bytes 6148
  898.3 447.4 %all-reduce.5.cloned.1.call-start = ((), (), s32[]{:S(2)}) async-start(), calls=%async_computation.15 | async-start | bytes 19660800 | tf_op jit(solution)/shard_map/psum | solution.py:210
  1149.8 6.9 copy-start.4
  1149.8 6.9 copy-start.15
  1149.8 6.9 copy-start.32
  1156.7 12.2 copy-start.24
  1156.7 62.8 %copy-start.21 = (f32[512]{0:T(512)S(1)}, f32[512]{0:T(512)}, u32[]{:S(2)}) copy-start(f32[512]{0:T(512)} %get-tuple-element.539) | copy-start | bytes 6148
  1345.6 7.5 slice-start.1
  1349.2 3.9 slice-start.2
  (27 other events, 53.3 us)
Sparse Core Ops, SparseCore 0:
  9.6 125.0 all-gather.5
  147.5 183.9 all-gather.7
  333.0 44.5 all-gather.9
  379.0 46.4 all-gather.11
  426.9 46.4 all-gather.13
  711.1 176.2 reduce-scatter.5
  890.2 45.8 reduce-scatter.11
  939.0 44.7 reduce-scatter.13
  986.6 44.7 reduce-scatter.9
  1034.3 114.7 reduce-scatter.7
  1153.1 192.5 all-reduce.4
